TPU v7x, 32 devices: a whole 2x2x4 slice. The times are simulated.
32 devices in a mesh: section: 8 (over z, y), rep: 4 (over x, core).
Axes of the slice: x: 2, y: 2, z: 4, core: 2. Of those that a mesh axis runs over, the one named last changes fastest.
Arguments:
- document_token_embedding: bfloat16 [8, 128, 4096], P('rep'), may hold values from -6 to 6
- doc_lengths: int32 [8, 4], P('rep'), may hold values from 1 to 32, as said below
- docid_embed: bfloat16 [8, 32, 4096], P('rep'), may hold values from -6 to 6
- docid_targets: int32 [8, 32], P('rep'), may hold values from 0 to 16383
- enc_gain: float32 [5, 4096], replicated, may hold values from 0.1 to 1.9
- dec_gain: float32 [2, 4096], replicated, may hold values from 0.1 to 1.9
- w_enc_qkv: bfloat16 [3, 12288, 4096], P(None, 'section'), may hold values from -0.03125 to 0.03125
- w_enc_out: bfloat16 [12288, 4096], P('section'), may hold values from -0.75 to 0.75
- cross_query_key_value_weight: bfloat16 [3, 4096, 4096], P(None, 'section'), may hold values from -0.03125 to 0.03125
- w_cross_out: bfloat16 [4096, 4096], P('section'), may hold values from -0.75 to 0.75
- docid_head_weight: bfloat16 [4096, 16384], P(None, 'section'), may hold values from -0.25 to 0.25
Outputs:
- logits: bfloat16 [8, 32, 16384], P('rep', None, 'section')
- token_loss: float32 [8, 32], P('rep')
- mean_loss: float32 [], replicated
Inputs may be any that keep to these rules, and one draw needn't show every extreme that they name: `doc_lengths`: in every draw some document has exactly 32 tokens.
All inputs are finite; a program needn't handle non-finite values.
Results may differ from a plain program's by a relative error of at most 0.019.
Values may be sent and summed in bfloat16 or wider, within the bound.
A program may use at most 128 MiB of HBM per device.

v0:
```python
import jax
import jax.numpy as jnp
from jax import lax
from jax.sharding import PartitionSpec as P

HD = 64
GROUPS = 4


def from_partner(block, axis, distance):
    count = lax.axis_size(axis)
    route = []
    for low in range(count):
        high = low | 1 << distance
        if high != low and high < count:
            route += [(low, high), (high, low)]
    return lax.ppermute(block, axis, route)


def from_behind(block, axis, distance):
    devices = range(lax.axis_size(axis))
    route = [(i - distance, i) for i in devices if i - distance in devices]
    return lax.ppermute(block, axis, route)


def passed_along(shard, axis, by):
    size = lax.axis_size(axis)
    return lax.ppermute(shard, axis, [(i, (i + by) % size) for i in range(size)])


def norm_rows(values, gain):
    values = values.astype(jnp.float32)
    scale = lax.rsqrt(jnp.mean(values * values, axis=-1, keepdims=True) + 1e-06)
    return values * scale * gain


def attend(queries, key_rows, values, allowed):
    scores = jnp.einsum("qhe,khe->hqk", queries, key_rows, preferred_element_type=jnp.float32)
    attention_weight_rows = jnp.where(allowed[None], jnp.exp(scores), 0.0)
    probabilities = (
        attention_weight_rows / jnp.sum(attention_weight_rows, axis=-1, keepdims=True)
    ).astype(jnp.bfloat16)
    mixture = jnp.einsum("hqk,khe->qhe", probabilities, values, preferred_element_type=jnp.float32)
    return mixture.astype(jnp.bfloat16)


def live_keys(lengths, key_doc, key_place):
    owners = jnp.arange(lengths.shape[0])
    matches = (key_doc[:, None] == owners[None, :]) & (key_place[:, None] < lengths[None, :])
    return jnp.any(matches, axis=1)


def lane_gather(own_rows, lane_bits, lane_index, concat_dim):
    for bit_number in range(lane_bits):
        partner = from_partner(own_rows, "section", bit_number)
        lower_half = lane_index // (1 << bit_number) % 2 == 0
        own_rows = jnp.where(
            lower_half,
            jnp.concatenate([own_rows, partner], concat_dim),
            jnp.concatenate([partner, own_rows], concat_dim),
        )
    return own_rows


def lane_reduce(totals, lane_bits, lane_index):
    for bit_number in reversed(range(lane_bits)):
        half_rows = totals.shape[0] // 2
        lower_half = lane_index // (1 << bit_number) % 2 == 0
        kept_rows = jnp.where(lower_half, totals[:half_rows], totals[half_rows:])
        outgoing = jnp.where(lower_half, totals[half_rows:], totals[:half_rows])
        totals = kept_rows + from_partner(outgoing, "section", bit_number)
    return totals


def relay_memory(encoder_memory, group_index, lane_count):
    encoder_memory = jnp.where(group_index == 0, encoder_memory, jnp.zeros_like(encoder_memory))
    for stride in (1, 2):
        encoder_memory = encoder_memory + from_behind(
            encoder_memory, "section", stride * lane_count
        )
    return encoder_memory


def shards(
    document_token_embedding,
    doc_lengths,
    docid_embed,
    docid_targets,
    enc_gain,
    dec_gain,
    w_enc_qkv,
    w_enc_out,
    cross_query_key_value_weight,
    w_cross_out,
    docid_head_weight,
):
    lane_count = lax.axis_size("section") // GROUPS
    lane_bits = lane_count.bit_length() - 1
    section_index = lax.axis_index("section")
    group_index = section_index // lane_count
    lane_index = section_index % lane_count
    micro_count, row_count, model_width = document_token_embedding.shape
    doc_count = doc_lengths.shape[1]
    doc_span = row_count // doc_count
    block_rows = row_count // lane_count
    local_heads = w_enc_qkv.shape[1] // HD
    positions = jnp.arange(row_count)
    key_doc = positions // doc_span
    key_place = positions % doc_span
    same_doc = key_doc[:, None] == key_doc[None, :]

    def partial_update(normed, lengths):
        allowed = same_doc & live_keys(lengths, key_doc, key_place)[None, :]
        projected = jnp.einsum(
            "rd,mcd->mrc", normed, w_enc_qkv, preferred_element_type=jnp.float32
        ).astype(jnp.bfloat16)
        projected = projected.reshape(3, row_count, local_heads, HD)
        mixture = attend(projected[0], projected[1], projected[2], allowed).reshape(row_count, -1)
        return jnp.dot(mixture, w_enc_out, preferred_element_type=jnp.float32)

    def section_step(step_index, loop_state):
        handed, encoder_memory = loop_state
        micro_index = step_index - group_index
        slot_index = jnp.clip(micro_index, 0, micro_count - 1)
        lengths = lax.dynamic_index_in_dim(doc_lengths, slot_index, 0, keepdims=False)
        layer_gain = lax.dynamic_index_in_dim(enc_gain, group_index, 0, keepdims=False)
        incoming = lax.dynamic_index_in_dim(
            document_token_embedding, jnp.minimum(step_index, micro_count - 1), 0, keepdims=False
        )
        incoming = lax.dynamic_slice_in_dim(incoming, lane_index * block_rows, block_rows, 0)
        current = jnp.where(group_index == 0, incoming, handed)
        normed = lane_gather(
            norm_rows(current, layer_gain).astype(jnp.bfloat16), lane_bits, lane_index, 0
        )
        summed = lane_reduce(partial_update(normed, lengths), lane_bits, lane_index)
        result = (current.astype(jnp.float32) + summed).astype(jnp.bfloat16)
        handed = passed_along(result, "section", lane_count)
        finished_index = step_index - (GROUPS - 1)
        finished_slot = jnp.clip(finished_index, 0, micro_count - 1)
        keeping = (group_index == 0) & (finished_index >= 0) & (finished_index < micro_count)
        stored = lax.dynamic_update_index_in_dim(encoder_memory, handed, finished_slot, 0)
        encoder_memory = jnp.where(keeping, stored, encoder_memory)
        return (handed, encoder_memory)

    handed = jnp.zeros((block_rows, model_width), jnp.bfloat16)
    encoder_memory = jnp.zeros((micro_count, block_rows, model_width), jnp.bfloat16)
    handed, encoder_memory = lax.fori_loop(
        0, micro_count + GROUPS - 1, section_step, (handed, encoder_memory)
    )
    encoder_memory = norm_rows(encoder_memory, enc_gain[GROUPS]).astype(jnp.bfloat16)
    encoder_memory = relay_memory(encoder_memory, group_index, lane_count)
    encoder_memory = lane_gather(encoder_memory, lane_bits, lane_index, 1)
    decoder_rows = docid_embed.shape[1]
    docid_span = decoder_rows // doc_count
    decoder_doc = jnp.arange(decoder_rows) // docid_span
    cross_heads = cross_query_key_value_weight.shape[1] // HD
    dec_normed = norm_rows(docid_embed, dec_gain[0]).astype(jnp.bfloat16)
    queries = jnp.einsum(
        "brd,cd->brc",
        dec_normed,
        cross_query_key_value_weight[0],
        preferred_element_type=jnp.float32,
    ).astype(jnp.bfloat16)
    memory_heads = jnp.einsum(
        "pye,qve->qpyv",
        encoder_memory,
        cross_query_key_value_weight[1:],
        preferred_element_type=jnp.float32,
    ).astype(jnp.bfloat16)

    def cross_one(sample_queries, sample_keys, sample_values, lengths):
        allowed = (decoder_doc[:, None] == key_doc[None, :]) & live_keys(
            lengths, key_doc, key_place
        )[None, :]
        return attend(sample_queries, sample_keys, sample_values, allowed)

    mixture = jax.vmap(cross_one)(
        queries.reshape(micro_count, decoder_rows, cross_heads, HD),
        memory_heads[0].reshape(micro_count, row_count, cross_heads, HD),
        memory_heads[1].reshape(micro_count, row_count, cross_heads, HD),
        doc_lengths,
    )
    cross_terms = jnp.einsum(
        "brc,cd->brd",
        mixture.reshape(micro_count, decoder_rows, -1),
        w_cross_out,
        preferred_element_type=jnp.float32,
    )
    cross_sum = lax.psum(cross_terms, "section")
    closing_rows = norm_rows(docid_embed.astype(jnp.float32) + cross_sum, dec_gain[1]).astype(
        jnp.bfloat16
    )
    scores_vocab = jnp.einsum(
        "brd,dv->brv", closing_rows, docid_head_weight, preferred_element_type=jnp.float32
    )
    vocab_local = docid_head_weight.shape[1]
    vocab_start = section_index * vocab_local
    matches = docid_targets[..., None] == vocab_start + jnp.arange(vocab_local)
    exponent_total, picked = lax.psum(
        (
            jnp.sum(jnp.exp(scores_vocab), axis=-1),
            jnp.sum(jnp.where(matches, scores_vocab, 0.0), axis=-1),
        ),
        "section",
    )
    token_loss = jnp.log(exponent_total) - picked
    mean_loss = lax.psum(jnp.sum(token_loss), "rep") / (token_loss.size * lax.axis_size("rep"))
    return (scores_vocab.astype(jnp.bfloat16), token_loss, mean_loss)


def solution(mesh):
    in_specs = (
        P("rep", None, None),
        P("rep", None),
        P("rep", None, None),
        P("rep", None),
        P(),
        P(),
        P(None, "section", None),
        P("section", None),
        P(None, "section", None),
        P("section", None),
        P(None, "section"),
    )
    out_specs = (P("rep", None, "section"), P("rep", None), P())
    return jax.shard_map(shards, mesh=mesh, in_specs=in_specs, out_specs=out_specs, check_vma=False)
```

profile of v0, /device:TPU:0, one launch (start us, length us, event | category | flops | bytes accessed | tf_op | source)
XLA Modules:
  0.0 631.1 jit_solution(10722782389679886046)
XLA Ops:
  9.1 407.9 %while.20 = (s32[]{:T(128)}, bf16[64,4096]{1,0:T(8,128)(2,1)S(1)}, bf16[2,64,4096]{2,1,0:T(8,128)(2,1)S(1)}, pred[]{:T(512)}, bf16[2,128,4096]{2,1,0:T(8,128)(2,...) while((s32[]{:T(128)}, bf16[64,4096]{1,0:T(8,128)(2,1)S(1)}, ...), condition=%wide.region_4.5_spmd.clone, body=%wide.region_0.4_spmd.clone.sunk | while | flops 6553770496 | bytes 86561208 | solution.py:147
  14.0 11.7 %collective-permute-done = bf16[64,4096]{1,0:T(8,128)(2,1)S(1)} collective-permute-done((bf16[64,4096]{1,0:T(8,128)(2,1)S(1)}, bf16[64,4096]{1,0:T(8,128)(2,1)S(1)}, u32[]{:S(2)}, u32[]{:S(2)}) %collective-permute-start) | collective-permute-done | bytes 524320 | tf_op jit(solution)/shard_map/while/body/eval_jaxpr/ppermute | solution.py:17
  26.5 21.6 %fusion.121 = bf16[3,128,1536]{2,1,0:T(8,128)(2,1)S(1)} fusion(bf16[3,1536,4096]{2,1,0:T(8,128)(2,1)} %get-tuple-element.743, bf16[64,4096]{1,0:T(8,128)(2,1)} %copy-done, bf16[64,4096]{1,0:T(8,128)(2,1)S(1)} %fusion.120, pred[]{:T(512)} %get-tuple-element.741), kind=kOutput, calls=%fused_computation.4.clone.1 | convolution fusion | flops 4837146624 | bytes 39976960 | tf_op jit(solution)/shard_map/while/body/eval_jaxpr/rd,mcd->mrc/dot_general | solution.py:114
  65.0 22.6 %collective-permute-done.1 = f32[64,4096]{1,0:T(8,128)S(1)} collective-permute-done((f32[64,4096]{1,0:T(8,128)S(1)}, f32[64,4096]{1,0:T(8,128)S(1)}, u32[]{:S(2)}, u32[]{:S(2)}) %collective-permute-start.1) | collective-permute-done | bytes 1048608 | tf_op jit(solution)/shard_map/while/body/eval_jaxpr/ppermute | solution.py:17
  89.4 12.5 %collective-permute-done.2 = bf16[64,4096]{1,0:T(8,128)(2,1)S(1)} collective-permute-done((bf16[64,4096]{1,0:T(8,128)(2,1)S(1)}, bf16[64,4096]{1,0:T(8,128)(2,1)S(1)}, u32[]{:S(2)}, u32[]{:S(2)}) %collective-permute-start.2) | collective-permute-done | bytes 524320 | tf_op jit(solution)/shard_map/while/body/eval_jaxpr/ppermute | solution.py:28
  105.3 10.0 %collective-permute-done = bf16[64,4096]{1,0:T(8,128)(2,1)S(1)} collective-permute-done((bf16[64,4096]{1,0:T(8,128)(2,1)S(1)}, bf16[64,4096]{1,0:T(8,128)(2,1)S(1)}, u32[]{:S(2)}, u32[]{:S(2)}) %collective-permute-start) | collective-permute-done | bytes 524320 | tf_op jit(solution)/shard_map/while/body/eval_jaxpr/ppermute | solution.py:17
  116.0 21.6 %fusion.121 = bf16[3,128,1536]{2,1,0:T(8,128)(2,1)S(1)} fusion(bf16[3,1536,4096]{2,1,0:T(8,128)(2,1)} %get-tuple-element.743, bf16[64,4096]{1,0:T(8,128)(2,1)} %copy-done, bf16[64,4096]{1,0:T(8,128)(2,1)S(1)} %fusion.120, pred[]{:T(512)} %get-tuple-element.741), kind=kOutput, calls=%fused_computation.4.clone.1 | convolution fusion | flops 4837146624 | bytes 39976960 | tf_op jit(solution)/shard_map/while/body/eval_jaxpr/rd,mcd->mrc/dot_general | solution.py:114
  153.8 20.8 %collective-permute-done.1 = f32[64,4096]{1,0:T(8,128)S(1)} collective-permute-done((f32[64,4096]{1,0:T(8,128)S(1)}, f32[64,4096]{1,0:T(8,128)S(1)}, u32[]{:S(2)}, u32[]{:S(2)}) %collective-permute-start.1) | collective-permute-done | bytes 1048608 | tf_op jit(solution)/shard_map/while/body/eval_jaxpr/ppermute | solution.py:17
  174.9 11.4 %collective-permute-done.2 = bf16[64,4096]{1,0:T(8,128)(2,1)S(1)} collective-permute-done((bf16[64,4096]{1,0:T(8,128)(2,1)S(1)}, bf16[64,4096]{1,0:T(8,128)(2,1)S(1)}, u32[]{:S(2)}, u32[]{:S(2)}) %collective-permute-start.2) | collective-permute-done | bytes 524320 | tf_op jit(solution)/shard_map/while/body/eval_jaxpr/ppermute | solution.py:28
  198.2 21.6 %fusion.121 = bf16[3,128,1536]{2,1,0:T(8,128)(2,1)S(1)} fusion(bf16[3,1536,4096]{2,1,0:T(8,128)(2,1)} %get-tuple-element.743, bf16[64,4096]{1,0:T(8,128)(2,1)} %copy-done, bf16[64,4096]{1,0:T(8,128)(2,1)S(1)} %fusion.120, pred[]{:T(512)} %get-tuple-element.741), kind=kOutput, calls=%fused_computation.4.clone.1 | convolution fusion | flops 4837146624 | bytes 39976960 | tf_op jit(solution)/shard_map/while/body/eval_jaxpr/rd,mcd->mrc/dot_general | solution.py:114
  235.4 18.4 %collective-permute-done.1 = f32[64,4096]{1,0:T(8,128)S(1)} collective-permute-done((f32[64,4096]{1,0:T(8,128)S(1)}, f32[64,4096]{1,0:T(8,128)S(1)}, u32[]{:S(2)}, u32[]{:S(2)}) %collective-permute-start.1) | collective-permute-done | bytes 1048608 | tf_op jit(solution)/shard_map/while/body/eval_jaxpr/ppermute | solution.py:17
  254.2 10.9 %collective-permute-done.2 = bf16[64,4096]{1,0:T(8,128)(2,1)S(1)} collective-permute-done((bf16[64,4096]{1,0:T(8,128)(2,1)S(1)}, bf16[64,4096]{1,0:T(8,128)(2,1)S(1)}, u32[]{:S(2)}, u32[]{:S(2)}) %collective-permute-start.2) | collective-permute-done | bytes 524320 | tf_op jit(solution)/shard_map/while/body/eval_jaxpr/ppermute | solution.py:28
  277.0 21.6 %fusion.121 = bf16[3,128,1536]{2,1,0:T(8,128)(2,1)S(1)} fusion(bf16[3,1536,4096]{2,1,0:T(8,128)(2,1)} %get-tuple-element.743, bf16[64,4096]{1,0:T(8,128)(2,1)} %copy-done, bf16[64,4096]{1,0:T(8,128)(2,1)S(1)} %fusion.120, pred[]{:T(512)} %get-tuple-element.741), kind=kOutput, calls=%fused_computation.4.clone.1 | convolution fusion | flops 4837146624 | bytes 39976960 | tf_op jit(solution)/shard_map/while/body/eval_jaxpr/rd,mcd->mrc/dot_general | solution.py:114
  314.0 15.5 %collective-permute-done.1 = f32[64,4096]{1,0:T(8,128)S(1)} collective-permute-done((f32[64,4096]{1,0:T(8,128)S(1)}, f32[64,4096]{1,0:T(8,128)S(1)}, u32[]{:S(2)}, u32[]{:S(2)}) %collective-permute-start.1) | collective-permute-done | bytes 1048608 | tf_op jit(solution)/shard_map/while/body/eval_jaxpr/ppermute | solution.py:17
  329.8 10.9 %collective-permute-done.2 = bf16[64,4096]{1,0:T(8,128)(2,1)S(1)} collective-permute-done((bf16[64,4096]{1,0:T(8,128)(2,1)S(1)}, bf16[64,4096]{1,0:T(8,128)(2,1)S(1)}, u32[]{:S(2)}, u32[]{:S(2)}) %collective-permute-start.2) | collective-permute-done | bytes 524320 | tf_op jit(solution)/shard_map/while/body/eval_jaxpr/ppermute | solution.py:28
  352.7 21.6 %fusion.121 = bf16[3,128,1536]{2,1,0:T(8,128)(2,1)S(1)} fusion(bf16[3,1536,4096]{2,1,0:T(8,128)(2,1)} %get-tuple-element.743, bf16[64,4096]{1,0:T(8,128)(2,1)} %copy-done, bf16[64,4096]{1,0:T(8,128)(2,1)S(1)} %fusion.120, pred[]{:T(512)} %get-tuple-element.741), kind=kOutput, calls=%fused_computation.4.clone.1 | convolution fusion | flops 4837146624 | bytes 39976960 | tf_op jit(solution)/shard_map/while/body/eval_jaxpr/rd,mcd->mrc/dot_general | solution.py:114
  389.7 14.5 %collective-permute-done.1 = f32[64,4096]{1,0:T(8,128)S(1)} collective-permute-done((f32[64,4096]{1,0:T(8,128)S(1)}, f32[64,4096]{1,0:T(8,128)S(1)}, u32[]{:S(2)}, u32[]{:S(2)}) %collective-permute-start.1) | collective-permute-done | bytes 1048608 | tf_op jit(solution)/shard_map/while/body/eval_jaxpr/ppermute | solution.py:17
  404.5 12.3 %collective-permute-done.2 = bf16[64,4096]{1,0:T(8,128)(2,1)S(1)} collective-permute-done((bf16[64,4096]{1,0:T(8,128)(2,1)S(1)}, bf16[64,4096]{1,0:T(8,128)(2,1)S(1)}, u32[]{:S(2)}, u32[]{:S(2)}) %collective-permute-start.2) | collective-permute-done | bytes 524320 | tf_op jit(solution)/shard_map/while/body/eval_jaxpr/ppermute | solution.py:28
  422.4 22.3 %collective-permute-done.3 = bf16[2,64,4096]{2,1,0:T(8,128)(2,1)S(1)} collective-permute-done((bf16[2,64,4096]{2,1,0:T(8,128)(2,1)S(1)}, bf16[2,64,4096]{2,1,0:T(8,128)(2,1)S(1)}, u32[]{:S(2)}, u32[]{:S(2)}) %collective-permute-start.3) | collective-permute-done | bytes 1048608 | tf_op jit(solution)/shard_map/ppermute | solution.py:23
  445.2 13.6 %collective-permute-start.4 = (bf16[2,64,4096]{2,1,0:T(8,128)(2,1)S(1)}, bf16[2,64,4096]{2,1,0:T(8,128)(2,1)S(1)}, u32[]{:S(2)}, u32[]{:S(2)}) collective-permute-start(bf16[2,64,4096]{2,1,0:T(8,128)(2,1)S(1)} %fusion.93), channel_id=1, source_target_pairs={{0,16},{4,20},{8,24},{12,28},{1,17},{5,21},{9,25},{13,29},{2,18},{... | collective-permute-start | bytes 3145736 | tf_op jit(solution)/shard_map/ppermute | solution.py:23
  459.0 12.0 %collective-permute-done.4 = bf16[2,64,4096]{2,1,0:T(8,128)(2,1)S(1)} collective-permute-done((bf16[2,64,4096]{2,1,0:T(8,128)(2,1)S(1)}, bf16[2,64,4096]{2,1,0:T(8,128)(2,1)S(1)}, u32[]{:S(2)}, u32[]{:S(2)}) %collective-permute-start.4) | collective-permute-done | bytes 1048608 | tf_op jit(solution)/shard_map/ppermute | solution.py:23
  475.6 10.6 %collective-permute-done.5 = bf16[2,64,4096]{2,1,0:T(8,128)(2,1)S(1)} collective-permute-done((bf16[2,64,4096]{2,1,0:T(8,128)(2,1)S(1)}, bf16[2,64,4096]{2,1,0:T(8,128)(2,1)S(1)}, u32[]{:S(2)}, u32[]{:S(2)}) %collective-permute-start.5) | collective-permute-done | bytes 1048608 | tf_op jit(solution)/shard_map/ppermute | solution.py:17
  497.3 86.5 %all-reduce.3.cloned.1.call-done = f32[2,32,4096]{2,1,0:T(8,128)} async-done(((f32[2,32,4096]{2,1,0:T(8,128)}), f32[2,32,4096]{2,1,0:T(8,128)}) %all-reduce.3.cloned.1.call-update) | async-done | bytes 1048592 | tf_op jit(solution)/shard_map/psum | solution.py:189
  595.0 20.0 %all-reduce = (f32[2,32]{1,0:T(2,128)S(1)}, f32[2,32]{1,0:T(2,128)S(1)}) all-reduce(f32[2,32]{1,0:T(2,128)S(1)} %get-tuple-element.562, f32[2,32]{1,0:T(2,128)S(1)} %get-tuple-element.561), channel_id=1, replica_groups=mesh['section'=8,'rep'=4] {'section'}, use_global_device_ids=true, to_apply=%region_14.15 | all-reduce | flops 128 | bytes 1024 | tf_op jit(solution)/shard_map/psum | solution.py:199
  (174 shorter events, 169.8 us)
Async XLA Ops:
  7.2 576.6 %all-reduce.3.cloned.1.call-start = ((), (), s32[]{:S(2)}) async-start(), calls=%async_computation | async-start | bytes 2097152 | tf_op jit(solution)/shard_map/psum | solution.py:189
  9.1 408.3 %copy-start.3 = (f32[1,4096]{1,0:T(1,128)S(1)}, f32[1,4096]{1,0:T(1,128)}, u32[]{:S(2)}) copy-start(f32[1,4096]{1,0:T(1,128)} %get-tuple-element.603) | copy-start | bytes 49156
  9.1 4.7 copy-start.6
  10.8 15.0 %collective-permute-start = (bf16[64,4096]{1,0:T(8,128)(2,1)S(1)}, bf16[64,4096]{1,0:T(8,128)(2,1)S(1)}, u32[]{:S(2)}, u32[]{:S(2)}) collective-permute-start(bf16[64,4096]{1,0:T(8,128)(2,1)S(1)} %fusion.120), channel_id=1, source_target_pairs={{0,4},{4,0},{8,12},{12,8},{16,20},{20,16},{24,28},{28,24},{1,5},{5... | collective-permute-start | bytes 1572872 | tf_op jit(solution)/shard_map/while/body/eval_jaxpr/ppermute | solution.py:17
  63.2 24.4 %collective-permute-start.1 = (f32[64,4096]{1,0:T(8,128)S(1)}, f32[64,4096]{1,0:T(8,128)S(1)}, u32[]{:S(2)}, u32[]{:S(2)}) collective-permute-start(f32[64,4096]{1,0:T(8,128)S(1)} %slice_select_fusion.2), channel_id=1, source_target_pairs={{0,4},{4,0},{8,12},{12,8},{16,20},{20,16},{24,28},{28,24},{1,5},{5... | collective-permute-start | bytes 3145736 | tf_op jit(solution)/shard_map/while/body/eval_jaxpr/ppermute | solution.py:17
  87.8 14.1 %collective-permute-start.2 = (bf16[64,4096]{1,0:T(8,128)(2,1)S(1)}, bf16[64,4096]{1,0:T(8,128)(2,1)S(1)}, u32[]{:S(2)}, u32[]{:S(2)}) collective-permute-start(bf16[64,4096]{1,0:T(8,128)(2,1)S(1)} %fusion.126), channel_id=1, source_target_pairs={{0,8},{4,12},{8,16},{12,20},{16,24},{20,28},{24,0},{28,4},{1,9},{5... | collective-permute-start | bytes 1572872 | tf_op jit(solution)/shard_map/while/body/eval_jaxpr/ppermute | solution.py:28
  103.8 11.4 %collective-permute-start = (bf16[64,4096]{1,0:T(8,128)(2,1)S(1)}, bf16[64,4096]{1,0:T(8,128)(2,1)S(1)}, u32[]{:S(2)}, u32[]{:S(2)}) collective-permute-start(bf16[64,4096]{1,0:T(8,128)(2,1)S(1)} %fusion.120), channel_id=1, source_target_pairs={{0,4},{4,0},{8,12},{12,8},{16,20},{20,16},{24,28},{28,24},{1,5},{5... | collective-permute-start | bytes 1572872 | tf_op jit(solution)/shard_map/while/body/eval_jaxpr/ppermute | solution.py:17
  152.7 21.8 %collective-permute-start.1 = (f32[64,4096]{1,0:T(8,128)S(1)}, f32[64,4096]{1,0:T(8,128)S(1)}, u32[]{:S(2)}, u32[]{:S(2)}) collective-permute-start(f32[64,4096]{1,0:T(8,128)S(1)} %slice_select_fusion.2), channel_id=1, source_target_pairs={{0,4},{4,0},{8,12},{12,8},{16,20},{20,16},{24,28},{28,24},{1,5},{5... | collective-permute-start | bytes 3145736 | tf_op jit(solution)/shard_map/while/body/eval_jaxpr/ppermute | solution.py:17
  174.8 11.5 %collective-permute-start.2 = (bf16[64,4096]{1,0:T(8,128)(2,1)S(1)}, bf16[64,4096]{1,0:T(8,128)(2,1)S(1)}, u32[]{:S(2)}, u32[]{:S(2)}) collective-permute-start(bf16[64,4096]{1,0:T(8,128)(2,1)S(1)} %fusion.126), channel_id=1, source_target_pairs={{0,8},{4,12},{8,16},{12,20},{16,24},{20,28},{24,0},{28,4},{1,9},{5... | collective-permute-start | bytes 1572872 | tf_op jit(solution)/shard_map/while/body/eval_jaxpr/ppermute | solution.py:28
  188.1 9.2 %collective-permute-start = (bf16[64,4096]{1,0:T(8,128)(2,1)S(1)}, bf16[64,4096]{1,0:T(8,128)(2,1)S(1)}, u32[]{:S(2)}, u32[]{:S(2)}) collective-permute-start(bf16[64,4096]{1,0:T(8,128)(2,1)S(1)} %fusion.120), channel_id=1, source_target_pairs={{0,4},{4,0},{8,12},{12,8},{16,20},{20,16},{24,28},{28,24},{1,5},{5... | collective-permute-start | bytes 1572872 | tf_op jit(solution)/shard_map/while/body/eval_jaxpr/ppermute | solution.py:17
  234.9 19.0 %collective-permute-start.1 = (f32[64,4096]{1,0:T(8,128)S(1)}, f32[64,4096]{1,0:T(8,128)S(1)}, u32[]{:S(2)}, u32[]{:S(2)}) collective-permute-start(f32[64,4096]{1,0:T(8,128)S(1)} %slice_select_fusion.2), channel_id=1, source_target_pairs={{0,4},{4,0},{8,12},{12,8},{16,20},{20,16},{24,28},{28,24},{1,5},{5... | collective-permute-start | bytes 3145736 | tf_op jit(solution)/shard_map/while/body/eval_jaxpr/ppermute | solution.py:17
  254.1 11.0 %collective-permute-start.2 = (bf16[64,4096]{1,0:T(8,128)(2,1)S(1)}, bf16[64,4096]{1,0:T(8,128)(2,1)S(1)}, u32[]{:S(2)}, u32[]{:S(2)}) collective-permute-start(bf16[64,4096]{1,0:T(8,128)(2,1)S(1)} %fusion.126), channel_id=1, source_target_pairs={{0,8},{4,12},{8,16},{12,20},{16,24},{20,28},{24,0},{28,4},{1,9},{5... | collective-permute-start | bytes 1572872 | tf_op jit(solution)/shard_map/while/body/eval_jaxpr/ppermute | solution.py:28
  267.0 9.2 %collective-permute-start = (bf16[64,4096]{1,0:T(8,128)(2,1)S(1)}, bf16[64,4096]{1,0:T(8,128)(2,1)S(1)}, u32[]{:S(2)}, u32[]{:S(2)}) collective-permute-start(bf16[64,4096]{1,0:T(8,128)(2,1)S(1)} %fusion.120), channel_id=1, source_target_pairs={{0,4},{4,0},{8,12},{12,8},{16,20},{20,16},{24,28},{28,24},{1,5},{5... | collective-permute-start | bytes 1572872 | tf_op jit(solution)/shard_map/while/body/eval_jaxpr/ppermute | solution.py:17
  313.7 15.8 %collective-permute-start.1 = (f32[64,4096]{1,0:T(8,128)S(1)}, f32[64,4096]{1,0:T(8,128)S(1)}, u32[]{:S(2)}, u32[]{:S(2)}) collective-permute-start(f32[64,4096]{1,0:T(8,128)S(1)} %slice_select_fusion.2), channel_id=1, source_target_pairs={{0,4},{4,0},{8,12},{12,8},{16,20},{20,16},{24,28},{28,24},{1,5},{5... | collective-permute-start | bytes 3145736 | tf_op jit(solution)/shard_map/while/body/eval_jaxpr/ppermute | solution.py:17
  329.7 11.0 %collective-permute-start.2 = (bf16[64,4096]{1,0:T(8,128)(2,1)S(1)}, bf16[64,4096]{1,0:T(8,128)(2,1)S(1)}, u32[]{:S(2)}, u32[]{:S(2)}) collective-permute-start(bf16[64,4096]{1,0:T(8,128)(2,1)S(1)} %fusion.126), channel_id=1, source_target_pairs={{0,8},{4,12},{8,16},{12,20},{16,24},{20,28},{24,0},{28,4},{1,9},{5... | collective-permute-start | bytes 1572872 | tf_op jit(solution)/shard_map/while/body/eval_jaxpr/ppermute | solution.py:28
  342.6 9.2 %collective-permute-start = (bf16[64,4096]{1,0:T(8,128)(2,1)S(1)}, bf16[64,4096]{1,0:T(8,128)(2,1)S(1)}, u32[]{:S(2)}, u32[]{:S(2)}) collective-permute-start(bf16[64,4096]{1,0:T(8,128)(2,1)S(1)} %fusion.120), channel_id=1, source_target_pairs={{0,4},{4,0},{8,12},{12,8},{16,20},{20,16},{24,28},{28,24},{1,5},{5... | collective-permute-start | bytes 1572872 | tf_op jit(solution)/shard_map/while/body/eval_jaxpr/ppermute | solution.py:17
  389.3 14.9 %collective-permute-start.1 = (f32[64,4096]{1,0:T(8,128)S(1)}, f32[64,4096]{1,0:T(8,128)S(1)}, u32[]{:S(2)}, u32[]{:S(2)}) collective-permute-start(f32[64,4096]{1,0:T(8,128)S(1)} %slice_select_fusion.2), channel_id=1, source_target_pairs={{0,4},{4,0},{8,12},{12,8},{16,20},{20,16},{24,28},{28,24},{1,5},{5... | collective-permute-start | bytes 3145736 | tf_op jit(solution)/shard_map/while/body/eval_jaxpr/ppermute | solution.py:17
  404.5 12.4 %collective-permute-start.2 = (bf16[64,4096]{1,0:T(8,128)(2,1)S(1)}, bf16[64,4096]{1,0:T(8,128)(2,1)S(1)}, u32[]{:S(2)}, u32[]{:S(2)}) collective-permute-start(bf16[64,4096]{1,0:T(8,128)(2,1)S(1)} %fusion.126), channel_id=1, source_target_pairs={{0,8},{4,12},{8,16},{12,20},{16,24},{20,28},{24,0},{28,4},{1,9},{5... | collective-permute-start | bytes 1572872 | tf_op jit(solution)/shard_map/while/body/eval_jaxpr/ppermute | solution.py:28
  417.0 5.2 copy-start.1
  417.7 41.2 %copy-start.4 = (f32[2,4096]{1,0:T(2,128)S(1)}, f32[2,4096]{1,0:T(2,128)}, u32[]{:S(2)}) copy-start(f32[2,4096]{1,0:T(2,128)} %param.18) | copy-start | bytes 98308
  417.7 27.0 %collective-permute-start.3 = (bf16[2,64,4096]{2,1,0:T(8,128)(2,1)S(1)}, bf16[2,64,4096]{2,1,0:T(8,128)(2,1)S(1)}, u32[]{:S(2)}, u32[]{:S(2)}) collective-permute-start(bf16[2,64,4096]{2,1,0:T(8,128)(2,1)S(1)} %fusion.65), channel_id=1, source_target_pairs={{0,8},{4,12},{8,16},{12,20},{16,24},{20,28},{1,9},{5,13},{9,17},{1... | collective-permute-start | bytes 3145736 | tf_op jit(solution)/shard_map/ppermute | solution.py:23
  445.2 25.8 %collective-permute-start.4 = (bf16[2,64,4096]{2,1,0:T(8,128)(2,1)S(1)}, bf16[2,64,4096]{2,1,0:T(8,128)(2,1)S(1)}, u32[]{:S(2)}, u32[]{:S(2)}) collective-permute-start(bf16[2,64,4096]{2,1,0:T(8,128)(2,1)S(1)} %fusion.93), channel_id=1, source_target_pairs={{0,16},{4,20},{8,24},{12,28},{1,17},{5,21},{9,25},{13,29},{2,18},{... | collective-permute-start | bytes 3145736 | tf_op jit(solution)/shard_map/ppermute | solution.py:23
  471.3 14.9 %collective-permute-start.5 = (bf16[2,64,4096]{2,1,0:T(8,128)(2,1)S(1)}, bf16[2,64,4096]{2,1,0:T(8,128)(2,1)S(1)}, u32[]{:S(2)}, u32[]{:S(2)}) collective-permute-start(bf16[2,64,4096]{2,1,0:T(8,128)(2,1)S(1)} %add.233), channel_id=1, source_target_pairs={{0,4},{4,0},{8,12},{12,8},{16,20},{20,16},{24,28},{28,24},{1,5},{5... | collective-permute-start | bytes 3145736 | tf_op jit(solution)/shard_map/ppermute | solution.py:17
  497.2 88.1 %copy-start.5 = (s32[2,32]{1,0:T(2,128)S(1)}, s32[2,32]{1,0:T(2,128)}, u32[]{:S(2)}) copy-start(s32[2,32]{1,0:T(2,128)} %param.16) | copy-start | bytes 772
  (11 other events, 18.5 us)
Sparse Core Ops, SparseCore 0:
  497.4 86.3 all-reduce.2
where the time goes:
time: 633 us; the launch traced here: 631 us
  waiting for transfers between devices  329 us (52%)
  matrix products  183 us (29%)
  local copies, waits for them, and re-layouts  30 us (5%)
  starting transfers between devices  29.9 us (5%)
  blocking collectives  26.3 us (4%)
  other arithmetic  16.4 us (3%)
  between operations  16.1 us (3%)
    ppermute x11, waiting for transfers between devices, from_partner(): return lax.ppermute(block, axis, route)  150 us
    dot_general x5, matrix products, partial_update(): jnp.einsum('rd,mcd->mrc', normed, w_enc_qkv, preferred_element_type=jnp.f...  108 us
    psum x1, waiting for transfers between devices, shards(): cross_sum = lax.psum(cross_terms, 'section')  86.5 us
    ppermute x5, waiting for transfers between devices, passed_along(): lax.ppermute(shard, axis, [(i, (i + by) % size) for i in range(size)])  58.1 us
    ppermute x2, waiting for transfers between devices, from_behind(): return lax.ppermute(block, axis, route)  34.4 us
    dot_general x5, matrix products, partial_update(): return jnp.dot(mixture, w_enc_out, preferred_element_type=jnp.float32)  32 us
    psum x1, blocking collectives, shards(): lax.psum((jnp.sum(jnp.exp(scores_vocab), axis=-1), jnp.sum(jnp.where(matc...  20 us
    ppermute x2, starting transfers between devices, from_behind(): return lax.ppermute(block, axis, route)  18.1 us
  transfers between devices with their start and end apart: 19, of which 19 were waited for; matrix products, arithmetic and copies ran while one was open for 1% of the time, Pallas kernels for 0%

commit v1 on v0

--- a/solution.py
+++ b/solution.py
@@ -1,10 +1,17 @@
+import functools
+
 import jax
 import jax.numpy as jnp
 from jax import lax
+from jax.experimental import pallas as pl
+from jax.experimental.pallas import tpu as pltpu
 from jax.sharding import PartitionSpec as P
 
 HD = 64
 GROUPS = 4
+WTILE = 512
+PARTS = 4
+MESH = pl.DeviceIdType.MESH
 
 
 def from_partner(block, axis, distance):
@@ -208,6 +215,401 @@
     return (scores_vocab.astype(jnp.bfloat16), token_loss, mean_loss)
 
 
+def encoder_kernel(
+    sent,
+    x_ref,
+    gain_ref,
+    row_doc_ref,
+    key_doc_ref,
+    wqkv_ref,
+    wout_ref,
+    mem_ref,
+    wqkv_v,
+    wout_v,
+    hid,
+    work,
+    part,
+    qkv,
+    mix,
+    w_sem,
+    o_sem,
+    x_sem,
+    gs,
+    gr,
+    rs,
+    rr,
+    zs,
+    zr,
+    bs,
+    br,
+    ms,
+    mr,
+):
+    rows, width = hid.shape
+    half = sent // 2
+    columns = width // PARTS
+    tiles = wqkv_v.shape[0]
+    per = tiles // 3
+    section = lax.axis_index("section")
+    count = lax.axis_size("section")
+    group = section // 2
+    lane = section % 2
+    partner = section + 1 - 2 * lane
+    ahead = lax.rem(section + 2, count)
+    behind = lax.rem(section + count - 2, count)
+    own = pl.ds(pl.multiple_of(lane * half, 16), half)
+    other = pl.ds(pl.multiple_of((1 - lane) * half, 16), half)
+
+    def cols(c):
+        return pl.ds(pl.multiple_of(c * columns, columns), columns)
+
+    def weight_copy(j):
+        return pltpu.make_async_copy(
+            wqkv_ref.at[j // per, pl.ds((j % per) * WTILE, WTILE)], wqkv_v.at[j], w_sem.at[j]
+        )
+
+    def out_copy(c):
+        return pltpu.make_async_copy(wout_ref.at[:, cols(c)], wout_v.at[c], o_sem.at[c])
+
+    def remote(src, dst, send, recv, device):
+        return pltpu.make_async_remote_copy(
+            src_ref=src,
+            dst_ref=dst,
+            send_sem=send,
+            recv_sem=recv,
+            device_id={"section": device},
+            device_id_type=MESH,
+        )
+
+    def gather(c, block):
+        return remote(hid.at[block, cols(c)], hid.at[block, cols(c)], gs.at[c], gr.at[c], partner)
+
+    def reduce(c):
+        return remote(work.at[other, cols(c)], part.at[:, cols(c)], rs.at[c], rr.at[c], partner)
+
+    def hand(c):
+        return remote(hid.at[own, cols(c)], hid.at[own, cols(c)], zs.at[c], zr.at[c], ahead)
+
+    def back(c):
+        return remote(mem_ref.at[own, cols(c)], mem_ref.at[own, cols(c)], bs.at[c], br.at[c], behind)
+
+    def spread(c, block):
+        return remote(
+            mem_ref.at[block, cols(c)], mem_ref.at[block, cols(c)], ms.at[c], mr.at[c], partner
+        )
+
+    def each(size, body):
+        def step(i, carry):
+            body(i)
+            return carry
+
+        lax.fori_loop(0, size, step, 0)
+
+    entry = pltpu.make_async_copy(x_ref.at[pl.ds(0, sent)], hid.at[pl.ds(0, sent)], x_sem)
+
+    @pl.when(group == 0)
+    def _():
+        entry.start()
+
+    for j in range(tiles):
+        weight_copy(j).start()
+    for c in range(PARTS):
+        out_copy(c).start()
+
+    barrier = pltpu.get_barrier_semaphore()
+    for device in (partner, ahead, behind):
+        pl.semaphore_signal(barrier, inc=1, device_id={"section": device}, device_id_type=MESH)
+    pl.semaphore_wait(barrier, 3)
+
+    if sent < rows:
+        hid[sent:, :] = jnp.zeros((rows - sent, width), hid.dtype)
+    if sent < mem_ref.shape[0]:
+        mem_ref[sent:, :] = jnp.zeros((mem_ref.shape[0] - sent, width), mem_ref.dtype)
+
+    @pl.when(group == 0)
+    def _():
+        entry.wait()
+
+    @pl.when(group > 0)
+    def _():
+        def arrive(c):
+            hand(c).wait_recv()
+            gather(c, own).start()
+
+        each(PARTS, arrive)
+
+        def complete(c):
+            gather(c, other).wait_recv()
+            gather(c, own).wait_send()
+
+        each(PARTS, complete)
+
+    def norm(r):
+        block = pl.ds(pl.multiple_of(r * 16, 16), 16)
+        values = hid[block, :].astype(jnp.float32)
+        scale = lax.rsqrt(jnp.mean(values * values, axis=-1, keepdims=True) + 1e-06)
+        work[block, :] = (values * scale * gain_ref[...]).astype(work.dtype)
+
+    each(rows // 16, norm)
+
+    def project(j):
+        pltpu.make_async_copy(
+            wqkv_ref.at[0, pl.ds(0, WTILE)], wqkv_v.at[j], w_sem.at[j]
+        ).wait()
+        qkv[j] = lax.dot_general(
+            work[...], wqkv_v[j], (((1,), (1,)), ((), ())), preferred_element_type=jnp.float32
+        ).astype(qkv.dtype)
+
+    each(tiles, project)
+    pairs = WTILE // (2 * HD)
+
+    def attend_pair(p):
+        tile = p // pairs
+        span = pl.ds(pl.multiple_of((p % pairs) * 2 * HD, 2 * HD), 2 * HD)
+        queries = qkv[tile, :, span]
+        keys = qkv[per + tile, :, span]
+        values = qkv[2 * per + tile, :, span]
+        allowed = row_doc_ref[...] == key_doc_ref[...]
+        first = lax.broadcasted_iota(jnp.int32, (rows, 2 * HD), 1) < HD
+        mixed = []
+        for side in range(2):
+            keep = first if side == 0 else jnp.logical_not(first)
+            chosen = jnp.where(keep, queries.astype(jnp.float32), 0.0).astype(jnp.bfloat16)
+            scores = lax.dot_general(
+                chosen, keys, (((1,), (1,)), ((), ())), preferred_element_type=jnp.float32
+            )
+            weights = jnp.where(allowed, jnp.exp(scores), 0.0)
+            shares = (weights / jnp.sum(weights, axis=-1, keepdims=True)).astype(jnp.bfloat16)
+            mixed.append(jnp.dot(shares, values, preferred_element_type=jnp.float32))
+        mix[:, pl.ds(pl.multiple_of(p * 2 * HD, 2 * HD), 2 * HD)] = jnp.where(
+            first, mixed[0], mixed[1]
+        ).astype(mix.dtype)
+
+    each(per * pairs, attend_pair)
+
+    def output(c):
+        out_copy(c).wait()
+        work[:, cols(c)] = jnp.dot(
+            mix[...], wout_v[c], preferred_element_type=jnp.float32
+        ).astype(work.dtype)
+        reduce(c).start()
+
+    each(PARTS, output)
+
+    def total(c):
+        reduce(c).wait_recv()
+        return (
+            hid[own, cols(c)].astype(jnp.float32)
+            + work[own, cols(c)].astype(jnp.float32)
+            + part[:, cols(c)].astype(jnp.float32)
+        ).astype(hid.dtype)
+
+    @pl.when(group < GROUPS - 1)
+    def _():
+        def finish(c):
+            hid[own, cols(c)] = total(c)
+            hand(c).start()
+
+        each(PARTS, finish)
+
+        def relay(c):
+            back(c).wait_recv()
+
+            @pl.when(group > 0)
+            def _():
+                back(c).start()
+
+            spread(c, own).start()
+
+        each(PARTS, relay)
+
+    @pl.when(group == GROUPS - 1)
+    def _():
+        def finish(c):
+            mem_ref[own, cols(c)] = total(c)
+            back(c).start()
+            spread(c, own).start()
+
+        each(PARTS, finish)
+
+    def drain(c):
+        spread(c, other).wait_recv()
+        spread(c, own).wait_send()
+        reduce(c).wait_send()
+
+        @pl.when(group < GROUPS - 1)
+        def _():
+            hand(c).wait_send()
+
+        @pl.when(group > 0)
+        def _():
+            back(c).wait_send()
+
+    each(PARTS, drain)
+
+
+def encode(rows, sent, number, x, gain, row_doc, key_doc, wqkv, wout):
+    total_rows, width = x.shape
+    inner = wout.shape[0]
+    tiles = 3 * (inner // WTILE)
+    dma = pltpu.SemaphoreType.DMA
+    vmem = pl.BlockSpec(memory_space=pltpu.VMEM)
+    anywhere = pl.BlockSpec(memory_space=pl.ANY)
+    return pl.pallas_call(
+        functools.partial(encoder_kernel, sent),
+        out_shape=jax.ShapeDtypeStruct((total_rows, width), jnp.bfloat16),
+        in_specs=[anywhere, vmem, vmem, vmem, anywhere, anywhere],
+        out_specs=vmem,
+        scratch_shapes=[
+            pltpu.VMEM((tiles, WTILE, width), jnp.bfloat16),
+            pltpu.VMEM((PARTS, inner, width // PARTS), jnp.bfloat16),
+            pltpu.VMEM((rows, width), jnp.bfloat16),
+            pltpu.VMEM((rows, width), jnp.bfloat16),
+            pltpu.VMEM((sent // 2, width), jnp.bfloat16),
+            pltpu.VMEM((tiles, rows, WTILE), jnp.bfloat16),
+            pltpu.VMEM((rows, inner), jnp.bfloat16),
+            dma((tiles,)),
+            dma((PARTS,)),
+            dma,
+        ]
+        + [dma((PARTS,))] * 10,
+        compiler_params=pltpu.CompilerParams(
+            collective_id=number, has_side_effects=True, vmem_limit_bytes=67043328
+        ),
+        name=f"encoder_{sent}",
+    )(x, gain, row_doc[:rows, None], key_doc[None, :rows], wqkv, wout)
+
+
+def butterfly(value, axis, combine):
+    for bit in range(lax.axis_size(axis).bit_length() - 1):
+        value = combine(value, from_partner(value, axis, bit))
+    return value
+
+
+def halves_reduced(totals, bits, index):
+    for bit in bits:
+        half = totals.shape[0] // 2
+        lower = index // (1 << bit) % 2 == 0
+        kept = jnp.where(lower, totals[:half], totals[half:])
+        outgoing = jnp.where(lower, totals[half:], totals[:half]).astype(jnp.bfloat16)
+        totals = kept + from_partner(outgoing, "section", bit).astype(jnp.float32)
+    return totals
+
+
+def halves_gathered(rows, bits, index):
+    for bit in bits:
+        partner = from_partner(rows, "section", bit)
+        lower = index // (1 << bit) % 2 == 0
+        rows = jnp.where(
+            lower, jnp.concatenate([rows, partner], 0), jnp.concatenate([partner, rows], 0)
+        )
+    return rows
+
+
+def own_rows(rows, bits, index):
+    for bit in bits:
+        half = rows.shape[0] // 2
+        lower = index // (1 << bit) % 2 == 0
+        rows = jnp.where(lower, rows[:half], rows[half:])
+    return rows
+
+
+def fast_shards(
+    document_token_embedding,
+    doc_lengths,
+    docid_embed,
+    docid_targets,
+    enc_gain,
+    dec_gain,
+    w_enc_qkv,
+    w_enc_out,
+    cross_query_key_value_weight,
+    w_cross_out,
+    docid_head_weight,
+):
+    section_index = lax.axis_index("section")
+    group_index = section_index // 2
+    micro_count, row_count, width = document_token_embedding.shape
+    doc_count = doc_lengths.shape[1]
+    doc_span = row_count // doc_count
+    all_rows = micro_count * row_count
+    positions = jnp.arange(all_rows)
+    lengths = doc_lengths.reshape(-1)
+    live = (jnp.arange(doc_span)[None, :] < lengths[:, None]).reshape(-1)
+    ends = jnp.cumsum(lengths)
+    live_count = ends[-1]
+    starts = jnp.concatenate([jnp.zeros((1,), ends.dtype), ends[:-1]])
+    inside = (positions[:, None] >= starts[None, :]) & (positions[:, None] < ends[None, :])
+    docs = jnp.arange(lengths.shape[0])
+    row_doc = jnp.sum(jnp.where(inside, docs[None, :], 0), axis=1).astype(jnp.int32)
+    key_doc = jnp.where(positions < live_count, row_doc, -1).astype(jnp.int32)
+    source = jnp.sum(
+        jnp.where(inside, docs[None, :] * doc_span + positions[:, None] - starts[None, :], 0), axis=1
+    )
+    source = jnp.where(positions < live_count, source, -1)
+    pick = (source[:, None] == positions[None, :]).astype(jnp.bfloat16)
+    packed = jnp.dot(
+        pick,
+        document_token_embedding.reshape(all_rows, width),
+        preferred_element_type=jnp.float32,
+    ).astype(jnp.bfloat16)
+    largest = butterfly(live_count.astype(jnp.float32)[None], "rep", jnp.maximum)[0]
+    gain = lax.dynamic_slice_in_dim(enc_gain, group_index, 1, 0)
+    unit = all_rows // 2
+    sizes = [(unit, unit * 3 // 4), (unit, unit), (all_rows, all_rows)]
+    choice = jnp.sum(jnp.stack([(largest > sent).astype(jnp.int32) for _, sent in sizes[:-1]]))
+    branches = [
+        functools.partial(encode, rows, sent, number) for number, (rows, sent) in enumerate(sizes)
+    ]
+    hidden = lax.switch(
+        choice, branches, packed, gain, row_doc, key_doc, w_enc_qkv, w_enc_out
+    )
+    memory = norm_rows(hidden, enc_gain[GROUPS]).astype(jnp.bfloat16)
+
+    decoder_rows = docid_embed.shape[1]
+    every = micro_count * decoder_rows
+    docid_span = decoder_rows // doc_count
+    decoder_doc = jnp.arange(every) // docid_span
+    cross_heads = cross_query_key_value_weight.shape[1] // HD
+    flat_docid = docid_embed.reshape(every, width)
+    dec_normed = norm_rows(flat_docid, dec_gain[0]).astype(jnp.bfloat16)
+
+    def project(values, weight):
+        return (
+            jnp.einsum("rd,cd->rc", values, weight, preferred_element_type=jnp.float32)
+            .astype(jnp.bfloat16)
+            .reshape(-1, cross_heads, HD)
+        )
+
+    queries = project(dec_normed, cross_query_key_value_weight[0])
+    keys = project(memory, cross_query_key_value_weight[1])
+    values = project(memory, cross_query_key_value_weight[2])
+    allowed = decoder_doc[:, None] == key_doc[None, :]
+    mixture = attend(queries, keys, values, allowed).reshape(every, -1)
+    cross_terms = jnp.dot(mixture, w_cross_out, preferred_element_type=jnp.float32)
+    bits = range(lax.axis_size("section").bit_length() - 1)
+    summed = halves_reduced(cross_terms, bits, section_index)
+    residual = own_rows(flat_docid, bits, section_index).astype(jnp.float32)
+    closing = norm_rows(residual + summed, dec_gain[1]).astype(jnp.bfloat16)
+    closing = halves_gathered(closing, reversed(bits), section_index)
+    scores_vocab = jnp.dot(closing, docid_head_weight, preferred_element_type=jnp.float32)
+    vocab_local = docid_head_weight.shape[1]
+    targets = docid_targets.reshape(-1)
+    matches = targets[:, None] == section_index * vocab_local + jnp.arange(vocab_local)
+    sums = jnp.stack(
+        [
+            jnp.sum(jnp.exp(scores_vocab), axis=-1),
+            jnp.sum(jnp.where(matches, scores_vocab, 0.0), axis=-1),
+        ]
+    )
+    sums = butterfly(sums, "section", jnp.add)
+    token_loss = jnp.log(sums[0]) - sums[1]
+    loss_sum = butterfly(jnp.sum(token_loss)[None], "rep", jnp.add)[0]
+    mean_loss = loss_sum / (token_loss.size * lax.axis_size("rep"))
+    logits = scores_vocab.astype(jnp.bfloat16).reshape(micro_count, decoder_rows, vocab_local)
+    return (logits, token_loss.reshape(docid_targets.shape), mean_loss)
+
+
 def solution(mesh):
     in_specs = (
         P("rep", None, None),
@@ -223,4 +625,5 @@
         P(None, "section"),
     )
     out_specs = (P("rep", None, "section"), P("rep", None), P())
-    return jax.shard_map(shards, mesh=mesh, in_specs=in_specs, out_specs=out_specs, check_vma=False)
+    local = shards if mesh.shape["section"] != 2 * GROUPS else fast_shards
+    return jax.shard_map(local, mesh=mesh, in_specs=in_specs, out_specs=out_specs, check_vma=False)

time: 633 us -> 291 us (0.46)
  waiting for transfers between devices: 329 us -> 48.2 us
  Pallas kernels: 0 us -> 184 us
  matrix products: 183 us -> 26.8 us
  blocking collectives: 26.3 us -> 0 us
  starting transfers between devices: 29.9 us -> 7.27 us
  local copies, waits for them, and re-layouts: 30 us -> 9.6 us
  between operations: 16.1 us -> 6.2 us
  other arithmetic: 16.4 us -> 8.74 us
    pallas_call x0 -> x1, Pallas kernels: none -> 184 us  [encode(): pl.pallas_call(functools.partial(encoder_kernel, sent), out_shape=jax.Sha...]
    dot_general x14 -> x6, matrix products: 163 us -> 26.2 us  [the longest x3 11.4 us: project(): jnp.einsum('rd,cd->rc', values, weight, preferred_element_type=jnp.float32)]
    ppermute x11 -> x13, waiting for transfers between devices: 150 us -> 48.2 us  [from_partner(): return lax.ppermute(block, axis, route)]
    ppermute x7 -> x0, waiting for transfers between devices: 92.5 us -> none  [the longest x5 58.1 us: passed_along(): lax.ppermute(shard, axis, [(i, (i + by) % size) for i in range(size)])]
    psum x1 -> x0, waiting for transfers between devices: 86.5 us -> none  [shards(): cross_sum = lax.psum(cross_terms, 'section')]
    psum x2 -> x0, blocking collectives: 26.3 us -> none  [the longest x1 20 us: shards(): lax.psum((jnp.sum(jnp.exp(scores_vocab), axis=-1), jnp.sum(jnp.where(matc...]
    slice x25 -> x4, local copies, waits for them, and re-layouts: 25.5 us -> 3.57 us  [the longest x1 1.52 us: fast_shards(): memory = norm_rows(hidden, enc_gain[GROUPS]).astype(jnp.bfloat16)]
    ppermute x7 -> x0, starting transfers between devices: 19.9 us -> none  [the longest x2 18.1 us: from_behind(): return lax.ppermute(block, axis, route)]
  transfers between devices with their start and end apart: 19 -> 13, of which waited for: 19 -> 12; matrix products, arithmetic and copies ran while one was open for 1% -> 5% of each run, Pallas kernels for 0% -> 0%
where the time goes in v1:
time: 291 us
  Pallas kernels  184 us (63%)
  waiting for transfers between devices  48.2 us (17%)
  matrix products  26.8 us (9%)
  local copies, waits for them, and re-layouts  9.6 us (3%)
  other arithmetic  8.74 us (3%)
  starting transfers between devices  7.27 us (2%)
  between operations  6.2 us (2%)
    pallas_call x1, Pallas kernels, encode(): pl.pallas_call(functools.partial(encoder_kernel, sent), out_shape=jax.Sha...  184 us
    ppermute x13, waiting for transfers between devices, from_partner(): return lax.ppermute(block, axis, route)  48.2 us
    dot_general x3, matrix products, project(): jnp.einsum('rd,cd->rc', values, weight, preferred_element_type=jnp.float32)  11.4 us
    dot_general x1, matrix products, fast_shards(): jnp.dot(closing, docid_head_weight, preferred_element_type=jnp.float32)  9.64 us
    ppermute x13, starting transfers between devices, from_partner(): return lax.ppermute(block, axis, route)  7.27 us
  transfers between devices with their start and end apart: 13, of which 12 were waited for; matrix products, arithmetic and copies ran while one was open for 5% of the time, Pallas kernels for 0%

profile of v1, /device:TPU:0, one launch (start us, length us, event | category | flops | bytes accessed | tf_op | source)
XLA Modules:
  0.0 290.9 jit_solution(13180502499111855175)
XLA Ops:
  3.0 1.4 collective-permute-start
  4.4 1.5 slice.107
  5.9 1.5 fusion.45
  9.8 3.6 %fusion.16 = bf16[64,512]{1,0:T(8,128)(2,1)S(1)} fusion(bf16[64,4096]{1,0:T(8,128)(2,1)S(1)} %bitcast.66, bf16[3,512,4096]{2,1,0:T(8,128)(2,1)} %param.22), kind=kOutput, calls=%fused_computation.31 | convolution fusion | flops 268468224 | bytes 4784128 | tf_op jit(solution)/shard_map/rd,cd->rc/dot_general | solution.py:579
  15.0 2.1 convolution_convert_fusion
  18.5 3.8 %collective-permute-start.1 = (f32[1]{0:T(128)}, f32[1]{0:T(128)}, u32[]{:S(2)}, u32[]{:S(2)}) collective-permute-start(f32[1]{0:T(128)} %max.6), channel_id=1, source_target_pairs={{0,2},{2,0},{1,3},{3,1},{4,6},{6,4},{5,7},{7,5},{8,10},{10,8},{9,1... | collective-permute-start | bytes 20 | tf_op jit(solution)/shard_map/ppermute | solution.py:24
  23.2 189.6 %conditional.2 = (bf16[256,4096]{1,0:T(8,128)(2,1)}, f32[256,1]{0,1:T(1,128)S(1)}) conditional(s32[]{:T(128)} %bitcast.12, (s32[]{:T(128)}, f32[5,4096]{1,0:T(8,128)}, s32[256]{0:T(256)S(1)}, s32[]{:T(128)}, s32[256]{0:T(256)S(1)}, /*index=5*/bf16[256,4096]{1,0:T(8,128)(2,1)}, bf16[3,1536,4096]{2,1,0:T(8,128)(2,1)}, ...), branch_computations={%region_3.5_spmd, %region_5.7_spmd, %region_7.9_spmd} | conditional | flops 3145987 | bytes 2137146
  23.3 1.5 constant_dynamic-slice_fusion.gain_ref
  26.7 183.9 %encoder_96.2 = bf16[256,4096]{1,0:T(8,128)(2,1)} custom-call(bf16[256,4096]{1,0:T(8,128)(2,1)} %get-tuple-element.168.x_ref, f32[1,4096]{1,0:T(1,128)} %constant_dynamic-slice_fusion.gain_ref, s32[128,1]{1,0:T(8,128)} %copy.25.row_doc_ref, s32[1,128]{1,0:T(1,128)} %slice_bitcast_fusion.key_doc_ref, bf16[3,1536,4096]{2,1,0:T(8,128)(2,1)} %get-tuple-element.174.wqkv_ref, ...), custom_call_target="tpu_custom_call" | custom-call | tf_op jit(solution)/shard_map/cond/branch_0_fun/encoder_96/pallas_call | solution.py:458
  210.6 2.1 multiply_reduce_fusion
  212.9 4.3 %fusion.13 = bf16[256,512]{1,0:T(8,128)(2,1)S(1)} fusion(bf16[3,512,4096]{2,1,0:T(8,128)(2,1)} %param.22, bf16[256,4096]{1,0:T(8,128)(2,1)} %get-tuple-element.197, f32[4096]{0:T(1024)} %bitcast.73, f32[256]{0:T(256)S(1)} %bitcast.85), kind=kOutput, calls=%fused_computation.29 | convolution fusion | flops 1078067200 | bytes 6571008 | tf_op jit(solution)/shard_map/rd,cd->rc/dot_general | solution.py:579
  217.2 3.5 %fusion.10 = bf16[256,512]{1,0:T(8,128)(2,1)S(1)} fusion(bf16[3,512,4096]{2,1,0:T(8,128)(2,1)} %param.22, bf16[256,4096]{1,0:T(8,128)(2,1)S(1)} %copy-done, f32[4096]{0:T(1024)S(1)} %bitcast.74, f32[256]{0:T(256)S(1)} %bitcast.86), kind=kOutput, calls=%fused_computation.28 | convolution fusion | flops 1078067200 | bytes 6571008 | tf_op jit(solution)/shard_map/rd,cd->rc/dot_general | solution.py:579
  221.6 3.1 %fusion.46 = f32[64,4096]{1,0:T(8,128)S(1)} fusion(bf16[64,512]{0,1:T(8,128)(2,1)S(1)} %bitcast.69, bf16[512,4096]{1,0:T(8,128)(2,1)} %param.23), kind=kOutput, calls=%fused_computation.93 | convolution fusion | flops 268435456 | bytes 5308416 | tf_op jit(solution)/shard_map/dot_general | solution.py:589
  224.9 6.3 %collective-permute-done.2 = bf16[32,4096]{1,0:T(8,128)(2,1)S(1)} collective-permute-done((bf16[32,4096]{1,0:T(8,128)(2,1)S(1)}, bf16[32,4096]{1,0:T(8,128)(2,1)S(1)}, u32[]{:S(2)}, u32[]{:S(2)}) %collective-permute-start.2) | collective-permute-done | bytes 262176 | tf_op jit(solution)/shard_map/ppermute | solution.py:24
  231.5 5.3 %collective-permute-done.3 = bf16[16,4096]{1,0:T(8,128)(2,1)S(1)} collective-permute-done((bf16[16,4096]{1,0:T(8,128)(2,1)S(1)}, bf16[16,4096]{1,0:T(8,128)(2,1)S(1)}, u32[]{:S(2)}, u32[]{:S(2)}) %collective-permute-start.3) | collective-permute-done | bytes 131104 | tf_op jit(solution)/shard_map/ppermute | solution.py:24
  236.9 5.6 %collective-permute-done.4 = bf16[8,4096]{1,0:T(8,128)(2,1)S(1)} collective-permute-done((bf16[8,4096]{1,0:T(8,128)(2,1)S(1)}, bf16[8,4096]{1,0:T(8,128)(2,1)S(1)}, u32[]{:S(2)}, u32[]{:S(2)}) %collective-permute-start.4) | collective-permute-done | bytes 65568 | tf_op jit(solution)/shard_map/ppermute | solution.py:24
  242.8 5.2 %collective-permute-done.5 = bf16[8,4096]{1,0:T(8,128)(2,1)S(1)} collective-permute-done((bf16[8,4096]{1,0:T(8,128)(2,1)S(1)}, bf16[8,4096]{1,0:T(8,128)(2,1)S(1)}, u32[]{:S(2)}, u32[]{:S(2)}) %collective-permute-start.5) | collective-permute-done | bytes 65568 | tf_op jit(solution)/shard_map/ppermute | solution.py:24
  248.1 5.0 %collective-permute-done.6 = bf16[16,4096]{1,0:T(8,128)(2,1)S(1)} collective-permute-done((bf16[16,4096]{1,0:T(8,128)(2,1)S(1)}, bf16[16,4096]{1,0:T(8,128)(2,1)S(1)}, u32[]{:S(2)}, u32[]{:S(2)}) %collective-permute-start.6) | collective-permute-done | bytes 131104 | tf_op jit(solution)/shard_map/ppermute | solution.py:24
  253.3 6.3 %collective-permute-done.7 = bf16[32,4096]{1,0:T(8,128)(2,1)S(1)} collective-permute-done((bf16[32,4096]{1,0:T(8,128)(2,1)S(1)}, bf16[32,4096]{1,0:T(8,128)(2,1)S(1)}, u32[]{:S(2)}, u32[]{:S(2)}) %collective-permute-start.7) | collective-permute-done | bytes 262176 | tf_op jit(solution)/shard_map/ppermute | solution.py:24
  259.6 9.6 %exponential_reduce_fusion = (f32[64]{0:T(128)S(1)}, f32[64]{0:T(128)S(1)}, bf16[64,2048]{1,0:T(8,128)(2,1)}) fusion(s32[2048]{0:T(1024)S(1)} %iota_add_fusion, s32[64]{0:T(128)S(1)} %eq.79, bf16[4096,2048]{1,0:T(8,128)(2,1)} %param.24, bf16[32,4096]{1,0:T(8,128)(2,1)S(1)} %collective-permute-done.7, bf16[32,4096]{1,0:T(8,128)(2,1)S(1)} %maximum_select_fusion.2, ...), kind=kOutput, calls=%fused_computation.43 | convolution fusion | flops 1076756480 | bytes 17572608 | tf_op jit(solution)/shard_map/dot_general | solution.py:595
  269.3 3.5 %collective-permute-done.8 = f32[2,64]{1,0:T(2,128)S(1)} collective-permute-done((f32[2,64]{1,0:T(2,128)S(1)}, f32[2,64]{1,0:T(2,128)S(1)}, u32[]{:S(2)}, u32[]{:S(2)}) %collective-permute-start.8) | collective-permute-done | bytes 544 | tf_op jit(solution)/shard_map/ppermute | solution.py:24
  273.0 3.6 %collective-permute-done.9 = f32[2,64]{1,0:T(2,128)S(1)} collective-permute-done((f32[2,64]{1,0:T(2,128)S(1)}, f32[2,64]{1,0:T(2,128)S(1)}, u32[]{:S(2)}, u32[]{:S(2)}) %collective-permute-start.9) | collective-permute-done | bytes 544 | tf_op jit(solution)/shard_map/ppermute | solution.py:24
  276.6 4.5 %collective-permute-done.10 = f32[2,64]{1,0:T(2,128)S(1)} collective-permute-done((f32[2,64]{1,0:T(2,128)S(1)}, f32[2,64]{1,0:T(2,128)S(1)}, u32[]{:S(2)}, u32[]{:S(2)}) %collective-permute-start.10) | collective-permute-done | bytes 544 | tf_op jit(solution)/shard_map/ppermute | solution.py:24
  286.8 2.2 collective-permute-done.12
  (75 shorter events, 15.1 us)
Async XLA Ops:
  0.6 14.4 %copy-start.2 = (bf16[2,128,4096]{2,1,0:T(8,128)(2,1)S(1)}, bf16[2,128,4096]{2,1,0:T(8,128)(2,1)}, u32[]{:S(2)}) copy-start(bf16[2,128,4096]{2,1,0:T(8,128)(2,1)} %param.14) | copy-start | bytes 6291460
  3.0 14.9 %collective-permute-start = (f32[1]{0:T(128)}, f32[1]{0:T(128)}, u32[]{:S(2)}, u32[]{:S(2)}) collective-permute-start(f32[1]{0:T(128)} %bitcast.11), channel_id=1, source_target_pairs={{0,1},{1,0},{2,3},{3,2},{4,5},{5,4},{6,7},{7,6},{8,9},{9,8},{10,11... | collective-permute-start | bytes 20 | tf_op jit(solution)/shard_map/ppermute | solution.py:24
  18.5 4.0 %collective-permute-start.1 = (f32[1]{0:T(128)}, f32[1]{0:T(128)}, u32[]{:S(2)}, u32[]{:S(2)}) collective-permute-start(f32[1]{0:T(128)} %max.6), channel_id=1, source_target_pairs={{0,2},{2,0},{1,3},{3,1},{4,6},{6,4},{5,7},{7,5},{8,10},{10,8},{9,1... | collective-permute-start | bytes 20 | tf_op jit(solution)/shard_map/ppermute | solution.py:24
  212.9 4.3 %copy-start = (bf16[256,4096]{1,0:T(8,128)(2,1)S(1)}, bf16[256,4096]{1,0:T(8,128)(2,1)}, u32[]{:S(2)}) copy-start(bf16[256,4096]{1,0:T(8,128)(2,1)} %get-tuple-element.197) | copy-start | bytes 6291460
  212.9 4.3 %copy-start.6 = (f32[1,4096]{1,0:T(1,128)S(1)}, f32[1,4096]{1,0:T(1,128)}, u32[]{:S(2)}) copy-start(f32[1,4096]{1,0:T(1,128)} %slice.107) | copy-start | bytes 49156
  217.2 3.8 %copy-start.3 = (bf16[64,8,64]{2,1,0:T(8,128)(2,1)S(1)}, bf16[64,8,64]{2,1,0:T(8,128)(2,1)}, u32[]{:S(2)}) copy-start(bf16[64,8,64]{2,1,0:T(8,128)(2,1)} %reshape.180) | copy-start | bytes 196612
  217.2 3.8 %copy-start.4 = (pred[64,256]{1,0:T(8,128)(4,1)S(1)}, pred[64,256]{1,0:T(8,128)(4,1)}, u32[]{:S(2)}) copy-start(pred[64,256]{1,0:T(8,128)(4,1)} %broadcast_compare_fusion) | copy-start | bytes 49156
  221.6 9.8 %copy-start.1 = (bf16[2,32,4096]{2,1,0:T(8,128)(2,1)S(1)}, bf16[2,32,4096]{2,1,0:T(8,128)(2,1)}, u32[]{:S(2)}) copy-start(bf16[2,32,4096]{2,1,0:T(8,128)(2,1)} %param.16) | copy-start | bytes 1572868
  224.7 17.9 %copy-start.5 = (f32[1,4096]{1,0:T(1,128)S(1)}, f32[1,4096]{1,0:T(1,128)}, u32[]{:S(2)}) copy-start(f32[1,4096]{1,0:T(1,128)} %get-tuple-element.208) | copy-start | bytes 49156
  224.7 28.5 %copy-start.7 = (s32[2,32]{1,0:T(2,128)S(1)}, s32[2,32]{1,0:T(2,128)}, u32[]{:S(2)}) copy-start(s32[2,32]{1,0:T(2,128)} %param.17) | copy-start | bytes 772
  224.8 6.4 %collective-permute-start.2 = (bf16[32,4096]{1,0:T(8,128)(2,1)S(1)}, bf16[32,4096]{1,0:T(8,128)(2,1)S(1)}, u32[]{:S(2)}, u32[]{:S(2)}) collective-permute-start(bf16[32,4096]{1,0:T(8,128)(2,1)S(1)} %select_convert_fusion), channel_id=1, source_target_pairs={{0,4},{4,0},{8,12},{12,8},{16,20},{20,16},{24,28},{28,24},{1,5},{5... | collective-permute-start | bytes 786440 | tf_op jit(solution)/shard_map/ppermute | solution.py:24
  231.3 5.4 %collective-permute-start.3 = (bf16[16,4096]{1,0:T(8,128)(2,1)S(1)}, bf16[16,4096]{1,0:T(8,128)(2,1)S(1)}, u32[]{:S(2)}, u32[]{:S(2)}) collective-permute-start(bf16[16,4096]{1,0:T(8,128)(2,1)S(1)} %select_convert_fusion.1), channel_id=1, source_target_pairs={{0,8},{8,0},{4,12},{12,4},{16,24},{24,16},{20,28},{28,20},{1,9},{9... | collective-permute-start | bytes 393224 | tf_op jit(solution)/shard_map/ppermute | solution.py:24
  236.8 5.7 %collective-permute-start.4 = (bf16[8,4096]{1,0:T(8,128)(2,1)S(1)}, bf16[8,4096]{1,0:T(8,128)(2,1)S(1)}, u32[]{:S(2)}, u32[]{:S(2)}) collective-permute-start(bf16[8,4096]{1,0:T(8,128)(2,1)S(1)} %select_convert_fusion.2), channel_id=1, source_target_pairs={{0,16},{16,0},{4,20},{20,4},{8,24},{24,8},{12,28},{28,12},{1,17},{... | collective-permute-start | bytes 196616 | tf_op jit(solution)/shard_map/ppermute | solution.py:24
  242.8 5.3 %collective-permute-start.5 = (bf16[8,4096]{1,0:T(8,128)(2,1)S(1)}, bf16[8,4096]{1,0:T(8,128)(2,1)S(1)}, u32[]{:S(2)}, u32[]{:S(2)}) collective-permute-start(bf16[8,4096]{1,0:T(8,128)(2,1)S(1)} %multiply_convert_fusion.3), channel_id=1, source_target_pairs={{0,16},{16,0},{4,20},{20,4},{8,24},{24,8},{12,28},{28,12},{1,17},{... | collective-permute-start | bytes 196616 | tf_op jit(solution)/shard_map/ppermute | solution.py:24
  248.1 5.0 %collective-permute-start.6 = (bf16[16,4096]{1,0:T(8,128)(2,1)S(1)}, bf16[16,4096]{1,0:T(8,128)(2,1)S(1)}, u32[]{:S(2)}, u32[]{:S(2)}) collective-permute-start(bf16[16,4096]{1,0:T(8,128)(2,1)S(1)} %maximum_select_fusion.3), channel_id=1, source_target_pairs={{0,8},{8,0},{4,12},{12,4},{16,24},{24,16},{20,28},{28,20},{1,9},{9... | collective-permute-start | bytes 393224 | tf_op jit(solution)/shard_map/ppermute | solution.py:24
  253.1 6.4 %collective-permute-start.7 = (bf16[32,4096]{1,0:T(8,128)(2,1)S(1)}, bf16[32,4096]{1,0:T(8,128)(2,1)S(1)}, u32[]{:S(2)}, u32[]{:S(2)}) collective-permute-start(bf16[32,4096]{1,0:T(8,128)(2,1)S(1)} %maximum_select_fusion.2), channel_id=1, source_target_pairs={{0,4},{4,0},{8,12},{12,8},{16,20},{20,16},{24,28},{28,24},{1,5},{5... | collective-permute-start | bytes 786440 | tf_op jit(solution)/shard_map/ppermute | solution.py:24
  269.2 3.6 %collective-permute-start.8 = (f32[2,64]{1,0:T(2,128)S(1)}, f32[2,64]{1,0:T(2,128)S(1)}, u32[]{:S(2)}, u32[]{:S(2)}) collective-permute-start(f32[2,64]{1,0:T(2,128)S(1)} %pad_maximum_fusion), channel_id=1, source_target_pairs={{0,4},{4,0},{8,12},{12,8},{16,20},{20,16},{24,28},{28,24},{1,5},{5... | collective-permute-start | bytes 1544 | tf_op jit(solution)/shard_map/ppermute | solution.py:24
  272.9 3.6 %collective-permute-start.9 = (f32[2,64]{1,0:T(2,128)S(1)}, f32[2,64]{1,0:T(2,128)S(1)}, u32[]{:S(2)}, u32[]{:S(2)}) collective-permute-start(f32[2,64]{1,0:T(2,128)S(1)} %fusion.43), channel_id=1, source_target_pairs={{0,8},{8,0},{4,12},{12,4},{16,24},{24,16},{20,28},{28,20},{1,9},{9... | collective-permute-start | bytes 1544 | tf_op jit(solution)/shard_map/ppermute | solution.py:24
  276.5 4.5 %collective-permute-start.10 = (f32[2,64]{1,0:T(2,128)S(1)}, f32[2,64]{1,0:T(2,128)S(1)}, u32[]{:S(2)}, u32[]{:S(2)}) collective-permute-start(f32[2,64]{1,0:T(2,128)S(1)} %fusion.55), channel_id=1, source_target_pairs={{0,16},{16,0},{4,20},{20,4},{8,24},{24,8},{12,28},{28,12},{1,17},{... | collective-permute-start | bytes 1544 | tf_op jit(solution)/shard_map/ppermute | solution.py:24
  282.8 1.3 collective-permute-start.11
  285.5 3.6 %collective-permute-start.12 = (f32[1]{0:T(128)}, f32[1]{0:T(128)}, u32[]{:S(2)}, u32[]{:S(2)}) collective-permute-start(f32[1]{0:T(128)} %add.131), channel_id=1, source_target_pairs={{0,2},{2,0},{1,3},{3,1},{4,6},{6,4},{5,7},{7,5},{8,10},{10,8},{9,1... | collective-permute-start | bytes 20 | tf_op jit(solution)/shard_map/ppermute | solution.py:24

commit v2 on v1

--- a/solution.py
+++ b/solution.py
@@ -486,32 +486,104 @@
     return value
 
 
-def halves_reduced(totals, bits, index):
-    for bit in bits:
-        half = totals.shape[0] // 2
-        lower = index // (1 << bit) % 2 == 0
-        kept = jnp.where(lower, totals[:half], totals[half:])
-        outgoing = jnp.where(lower, totals[half:], totals[:half]).astype(jnp.bfloat16)
-        totals = kept + from_partner(outgoing, "section", bit).astype(jnp.float32)
-    return totals
-
-
-def halves_gathered(rows, bits, index):
-    for bit in bits:
-        partner = from_partner(rows, "section", bit)
-        lower = index // (1 << bit) % 2 == 0
-        rows = jnp.where(
-            lower, jnp.concatenate([rows, partner], 0), jnp.concatenate([partner, rows], 0)
-        )
-    return rows
-
-
-def own_rows(rows, bits, index):
-    for bit in bits:
-        half = rows.shape[0] // 2
-        lower = index // (1 << bit) % 2 == 0
-        rows = jnp.where(lower, rows[:half], rows[half:])
-    return rows
+def greet(me, count):
+    barrier = pltpu.get_barrier_semaphore()
+    for k in range(1, count):
+        pl.semaphore_signal(
+            barrier, inc=1, device_id={"section": lax.rem(me + k, count)}, device_id_type=MESH
+        )
+    pl.semaphore_wait(barrier, count - 1)
+
+
+def to_peer(src, dst, send, recv, peer):
+    return pltpu.make_async_remote_copy(
+        src_ref=src,
+        dst_ref=dst,
+        send_sem=send,
+        recv_sem=recv,
+        device_id={"section": peer},
+        device_id_type=MESH,
+    )
+
+
+def closing_kernel(terms, residual, gain, out, landed, s1, r1, s2, r2):
+    count = terms.shape[0]
+    me = lax.axis_index("section")
+    greet(me, count)
+
+    def scatter(k, slot):
+        peer = lax.rem(me + k, count)
+        return to_peer(terms.at[peer], landed.at[slot], s1.at[k], r1.at[k], peer)
+
+    def gather(k, slot):
+        return to_peer(out.at[slot], out.at[slot], s2.at[k], r2.at[k], lax.rem(me + k, count))
+
+    for k in range(1, count):
+        scatter(k, me).start()
+    total = residual[...] + terms[me].astype(jnp.float32)
+    for k in range(1, count):
+        slot = lax.rem(me + count - k, count)
+        scatter(k, slot).wait_recv()
+        total = total + landed[slot].astype(jnp.float32)
+    scale = lax.rsqrt(jnp.mean(total * total, axis=-1, keepdims=True) + 1e-06)
+    out[me] = (total * scale * gain[...]).astype(out.dtype)
+    for k in range(1, count):
+        gather(k, me).start()
+    for k in range(1, count):
+        gather(k, lax.rem(me + count - k, count)).wait_recv()
+    for k in range(1, count):
+        scatter(k, me).wait_send()
+        gather(k, me).wait_send()
+
+
+def closing_rows_of(terms, residual, gain):
+    count = terms.shape[0]
+    dma = pltpu.SemaphoreType.DMA
+    vmem = pl.BlockSpec(memory_space=pltpu.VMEM)
+    return pl.pallas_call(
+        closing_kernel,
+        out_shape=jax.ShapeDtypeStruct(terms.shape, jnp.bfloat16),
+        in_specs=[vmem] * 3,
+        out_specs=vmem,
+        scratch_shapes=[pltpu.VMEM(terms.shape, jnp.bfloat16)] + [dma((count,))] * 4,
+        compiler_params=pltpu.CompilerParams(collective_id=8, has_side_effects=True),
+        name="closing",
+    )(terms, residual, gain)
+
+
+def sums_kernel(value, out, landed, send, recv):
+    count = landed.shape[0]
+    me = lax.axis_index("section")
+    greet(me, count)
+
+    def share(k, slot):
+        return to_peer(value, landed.at[slot], send.at[k], recv.at[k], lax.rem(me + k, count))
+
+    for k in range(1, count):
+        share(k, me).start()
+    landed[me] = value[...]
+    for k in range(1, count):
+        share(k, lax.rem(me + count - k, count)).wait_recv()
+    total = landed[0]
+    for k in range(1, count):
+        total = total + landed[k]
+    out[...] = total
+    for k in range(1, count):
+        share(k, me).wait_send()
+
+
+def section_sum(value, count):
+    dma = pltpu.SemaphoreType.DMA
+    vmem = pl.BlockSpec(memory_space=pltpu.VMEM)
+    return pl.pallas_call(
+        sums_kernel,
+        out_shape=jax.ShapeDtypeStruct(value.shape, value.dtype),
+        in_specs=[vmem],
+        out_specs=vmem,
+        scratch_shapes=[pltpu.VMEM((count,) + value.shape, value.dtype)] + [dma((count,))] * 2,
+        compiler_params=pltpu.CompilerParams(collective_id=9, has_side_effects=True),
+        name="section_sum",
+    )(value)
 
 
 def fast_shards(
@@ -587,11 +659,14 @@
     allowed = decoder_doc[:, None] == key_doc[None, :]
     mixture = attend(queries, keys, values, allowed).reshape(every, -1)
     cross_terms = jnp.dot(mixture, w_cross_out, preferred_element_type=jnp.float32)
-    bits = range(lax.axis_size("section").bit_length() - 1)
-    summed = halves_reduced(cross_terms, bits, section_index)
-    residual = own_rows(flat_docid, bits, section_index).astype(jnp.float32)
-    closing = norm_rows(residual + summed, dec_gain[1]).astype(jnp.bfloat16)
-    closing = halves_gathered(closing, reversed(bits), section_index)
+    section_count = lax.axis_size("section")
+    share = every // section_count
+    residual = lax.dynamic_slice_in_dim(flat_docid, section_index * share, share, 0)
+    closing = closing_rows_of(
+        cross_terms.astype(jnp.bfloat16).reshape(section_count, share, width),
+        residual.astype(jnp.float32),
+        dec_gain[1:2],
+    ).reshape(every, width)
     scores_vocab = jnp.dot(closing, docid_head_weight, preferred_element_type=jnp.float32)
     vocab_local = docid_head_weight.shape[1]
     targets = docid_targets.reshape(-1)
@@ -602,7 +677,8 @@
             jnp.sum(jnp.where(matches, scores_vocab, 0.0), axis=-1),
         ]
     )
-    sums = butterfly(sums, "section", jnp.add)
+    padding = ((0, -sums.shape[0] % 8), (0, -sums.shape[1] % 128))
+    sums = section_sum(jnp.pad(sums, padding), section_count)[:2, :every]
     token_loss = jnp.log(sums[0]) - sums[1]
     loss_sum = butterfly(jnp.sum(token_loss)[None], "rep", jnp.add)[0]
     mean_loss = loss_sum / (token_loss.size * lax.axis_size("rep"))

time: 291 us -> 277 us (0.952)
  waiting for transfers between devices: 48.2 us -> 1.72 us
  Pallas kernels: 184 us -> 211 us
    ppermute x13 -> x4, waiting for transfers between devices: 48.2 us -> 1.72 us  [from_partner(): return lax.ppermute(block, axis, route)]
    pallas_call x0 -> x2, Pallas kernels: none -> 27.5 us  [the longest x1 18.6 us: closing_rows_of(): pl.pallas_call(closing_kernel, out_shape=jax.ShapeDtypeStruct(terms.shape...]
    ppermute x13 -> x4, starting transfers between devices: 7.27 us -> 8.21 us  [from_partner(): return lax.ppermute(block, axis, route)]
  transfers between devices with their start and end apart: 13 -> 4, of which waited for: 12 -> 3; matrix products, arithmetic and copies ran while one was open for 5% -> 6% of each run, Pallas kernels for 0% -> 0%
where the time goes in v2:
time: 277 us; the launch traced here: 276 us
  Pallas kernels  211 us (76%)
  matrix products  27.7 us (10%)
  other arithmetic  11.6 us (4%)
  local copies, waits for them, and re-layouts  10.2 us (4%)
  starting transfers between devices  8.21 us (3%)
  between operations  5.93 us (2%)
    pallas_call x1, Pallas kernels, encode(): pl.pallas_call(functools.partial(encoder_kernel, sent), out_shape=jax.Sha...  183 us
    pallas_call x1, Pallas kernels, closing_rows_of(): pl.pallas_call(closing_kernel, out_shape=jax.ShapeDtypeStruct(terms.shape...  18.6 us
    dot_general x3, matrix products, project(): jnp.einsum('rd,cd->rc', values, weight, preferred_element_type=jnp.float32)  11.4 us
    dot_general x1, matrix products, fast_shards(): jnp.dot(closing, docid_head_weight, preferred_element_type=jnp.float32)  9.83 us
    pallas_call x1, Pallas kernels, section_sum(): pl.pallas_call(sums_kernel, out_shape=jax.ShapeDtypeStruct(value.shape, v...  8.88 us
    ppermute x4, starting transfers between devices, from_partner(): return lax.ppermute(block, axis, route)  8.21 us
  transfers between devices with their start and end apart: 4, of which 3 were waited for; matrix products, arithmetic and copies ran while one was open for 6% of the time, Pallas kernels for 0%

profile of v2, /device:TPU:0, one launch (start us, length us, event | category | flops | bytes accessed | tf_op | source)
XLA Modules:
  0.0 276.0 jit_solution(7904434583991949260)
XLA Ops:
  0.7 0.9 reshape.163
  3.0 1.5 collective-permute-start
  4.6 1.5 slice.56
  6.1 1.5 fusion.38
  7.5 1.2 fusion.20
  8.8 1.2 fusion.22
  10.0 3.6 %fusion.17 = bf16[64,512]{1,0:T(8,128)(2,1)S(1)} fusion(bf16[64,4096]{1,0:T(8,128)(2,1)S(1)} %bitcast.68, bf16[3,512,4096]{2,1,0:T(8,128)(2,1)} %param.22), kind=kOutput, calls=%fused_computation.33 | convolution fusion | flops 268468224 | bytes 4784128 | tf_op jit(solution)/shard_map/rd,cd->rc/dot_general | solution.py:651
  13.6 0.8 reshape.166
  16.4 2.1 convolution_convert_fusion
  19.2 1.5 dynamic-slice_convert_fusion.residual
  21.3 3.8 %collective-permute-start.1 = (f32[1]{0:T(128)}, f32[1]{0:T(128)}, u32[]{:S(2)}, u32[]{:S(2)}) collective-permute-start(f32[1]{0:T(128)} %max.6), channel_id=1, source_target_pairs={{0,2},{2,0},{1,3},{3,1},{4,6},{6,4},{5,7},{7,5},{8,10},{10,8},{9,1... | collective-permute-start | bytes 20 | tf_op jit(solution)/shard_map/ppermute | solution.py:24
  26.2 188.7 %conditional.2 = (bf16[256,4096]{1,0:T(8,128)(2,1)}, f32[256,1]{0,1:T(1,128)S(1)}) conditional(s32[]{:T(128)} %bitcast.11, (s32[]{:T(128)}, f32[5,4096]{1,0:T(8,128)}, s32[256]{0:T(256)S(1)}, s32[]{:T(128)}, s32[256]{0:T(256)S(1)}, /*index=5*/bf16[256,4096]{1,0:T(8,128)(2,1)}, bf16[3,1536,4096]{2,1,0:T(8,128)(2,1)}, ...), branch_computations={%region_3.5_spmd, %region_5.7_spmd, %region_7.9_spmd} | conditional | flops 3145987 | bytes 2137146
  26.2 1.5 constant_dynamic-slice_fusion.gain_ref
  29.6 183.0 %encoder_96.2 = bf16[256,4096]{1,0:T(8,128)(2,1)} custom-call(bf16[256,4096]{1,0:T(8,128)(2,1)} %get-tuple-element.168.x_ref, f32[1,4096]{1,0:T(1,128)} %constant_dynamic-slice_fusion.gain_ref, s32[128,1]{1,0:T(8,128)} %copy.25.row_doc_ref, s32[1,128]{1,0:T(1,128)} %slice_bitcast_fusion.key_doc_ref, bf16[3,1536,4096]{2,1,0:T(8,128)(2,1)} %get-tuple-element.174.wqkv_ref, ...), custom_call_target="tpu_custom_call" | custom-call | tf_op jit(solution)/shard_map/cond/branch_0_fun/encoder_96/pallas_call | solution.py:458
  212.6 2.1 multiply_reduce_fusion
  214.9 4.3 %fusion.14 = bf16[256,512]{1,0:T(8,128)(2,1)S(1)} fusion(bf16[3,512,4096]{2,1,0:T(8,128)(2,1)} %param.22, bf16[256,4096]{1,0:T(8,128)(2,1)} %get-tuple-element.197, f32[4096]{0:T(1024)} %bitcast.74, f32[256]{0:T(256)S(1)} %bitcast.82), kind=kOutput, calls=%fused_computation.31 | convolution fusion | flops 1078067200 | bytes 6571008 | tf_op jit(solution)/shard_map/rd,cd->rc/dot_general | solution.py:651
  219.3 3.5 %fusion.11 = bf16[256,512]{1,0:T(8,128)(2,1)S(1)} fusion(bf16[3,512,4096]{2,1,0:T(8,128)(2,1)} %param.22, bf16[256,4096]{1,0:T(8,128)(2,1)S(1)} %copy-done, f32[4096]{0:T(1024)S(1)} %bitcast.75, f32[256]{0:T(256)S(1)} %bitcast.83), kind=kOutput, calls=%fused_computation.30 | convolution fusion | flops 1078067200 | bytes 6571008 | tf_op jit(solution)/shard_map/rd,cd->rc/dot_general | solution.py:651
  223.6 3.9 %fusion.terms = bf16[8,8,4096]{2,1,0:T(8,128)(2,1)} fusion(bf16[64,512]{0,1:T(8,128)(2,1)S(1)} %bitcast.71, bf16[512,4096]{1,0:T(8,128)(2,1)} %param.23), kind=kOutput, calls=%fused_computation.15 | convolution fusion | flops 268697600 | bytes 4784128 | tf_op jit(solution)/shard_map/dot_general | solution.py:661
  227.5 18.6 %closing.1 = bf16[8,8,4096]{2,1,0:T(8,128)(2,1)} custom-call(bf16[8,8,4096]{2,1,0:T(8,128)(2,1)} %fusion.terms, f32[8,4096]{1,0:T(8,128)} %dynamic-slice_convert_fusion.residual, f32[1,4096]{1,0:T(1,128)} %get-tuple-element.206.gain), custom_call_target="tpu_custom_call" | custom-call | tf_op jit(solution)/shard_map/closing/pallas_call | solution.py:543
  246.1 9.8 %exponential_reduce_fusion = (f32[64]{0:T(128)S(1)}, f32[64]{0:T(128)S(1)}, bf16[64,2048]{1,0:T(8,128)(2,1)}) fusion(s32[2048]{0:T(1024)S(1)} %copy-done.4, s32[64]{0:T(128)S(1)} %copy-done.6, bf16[4096,2048]{1,0:T(8,128)(2,1)} %param.24, bf16[8,8,4096]{2,1,0:T(8,128)(2,1)} %closing.1), kind=kOutput, calls=%fused_computation.40 | convolution fusion | flops 1074397184 | bytes 17572608 | tf_op jit(solution)/shard_map/dot_general | solution.py:670
  256.6 8.9 %section_sum.1 = f32[8,128]{1,0:T(8,128)} custom-call(f32[8,128]{1,0:T(8,128)} %select_maximum_fusion.value), custom_call_target="tpu_custom_call" | custom-call | tf_op jit(solution)/shard_map/section_sum/pallas_call | solution.py:578
  266.0 2.0 fusion.37
  270.6 2.9 %collective-permute-start.3 = (f32[1]{0:T(128)}, f32[1]{0:T(128)}, u32[]{:S(2)}, u32[]{:S(2)}) collective-permute-start(f32[1]{0:T(128)} %add.79), channel_id=1, source_target_pairs={{0,2},{2,0},{1,3},{3,1},{4,6},{6,4},{5,7},{7,5},{8,10},{10,8},{9,1... | collective-permute-start | bytes 20 | tf_op jit(solution)/shard_map/ppermute | solution.py:24
  273.5 0.7 collective-permute-done.3
  (45 shorter events, 9.0 us)
Async XLA Ops:
  0.6 14.4 %copy-start.7 = (s32[2,32]{1,0:T(2,128)S(1)}, s32[2,32]{1,0:T(2,128)}, u32[]{:S(2)}) copy-start(s32[2,32]{1,0:T(2,128)} %param.17) | copy-start | bytes 772
  0.6 15.8 %copy-start.1 = (bf16[2,128,4096]{2,1,0:T(8,128)(2,1)S(1)}, bf16[2,128,4096]{2,1,0:T(8,128)(2,1)}, u32[]{:S(2)}) copy-start(bf16[2,128,4096]{2,1,0:T(8,128)(2,1)} %param.14) | copy-start | bytes 6291460
  3.0 17.7 %collective-permute-start = (f32[1]{0:T(128)}, f32[1]{0:T(128)}, u32[]{:S(2)}, u32[]{:S(2)}) collective-permute-start(f32[1]{0:T(128)} %bitcast.10), channel_id=1, source_target_pairs={{0,1},{1,0},{2,3},{3,2},{4,5},{5,4},{6,7},{7,6},{8,9},{9,8},{10,11... | collective-permute-start | bytes 20 | tf_op jit(solution)/shard_map/ppermute | solution.py:24
  21.3 4.2 %collective-permute-start.1 = (f32[1]{0:T(128)}, f32[1]{0:T(128)}, u32[]{:S(2)}, u32[]{:S(2)}) collective-permute-start(f32[1]{0:T(128)} %max.6), channel_id=1, source_target_pairs={{0,2},{2,0},{1,3},{3,1},{4,6},{6,4},{5,7},{7,5},{8,10},{10,8},{9,1... | collective-permute-start | bytes 20 | tf_op jit(solution)/shard_map/ppermute | solution.py:24
  214.9 4.3 %copy-start = (bf16[256,4096]{1,0:T(8,128)(2,1)S(1)}, bf16[256,4096]{1,0:T(8,128)(2,1)}, u32[]{:S(2)}) copy-start(bf16[256,4096]{1,0:T(8,128)(2,1)} %get-tuple-element.197) | copy-start | bytes 6291460
  214.9 4.3 %copy-start.5 = (f32[1,4096]{1,0:T(1,128)S(1)}, f32[1,4096]{1,0:T(1,128)}, u32[]{:S(2)}) copy-start(f32[1,4096]{1,0:T(1,128)} %slice.56) | copy-start | bytes 49156
  219.2 3.8 %copy-start.2 = (bf16[64,8,64]{2,1,0:T(8,128)(2,1)S(1)}, bf16[64,8,64]{2,1,0:T(8,128)(2,1)}, u32[]{:S(2)}) copy-start(bf16[64,8,64]{2,1,0:T(8,128)(2,1)} %reshape.166) | copy-start | bytes 196612
  219.3 3.8 %copy-start.3 = (pred[64,256]{1,0:T(8,128)(4,1)S(1)}, pred[64,256]{1,0:T(8,128)(4,1)}, u32[]{:S(2)}) copy-start(pred[64,256]{1,0:T(8,128)(4,1)} %broadcast_compare_fusion) | copy-start | bytes 49156
  223.3 22.8 %copy-start.4 = (s32[2048]{0:T(1024)S(1)}, s32[2048]{0:T(1024)}, u32[]{:S(2)}) copy-start(s32[2048]{0:T(1024)} %iota_add_fusion) | copy-start | bytes 24580
  223.3 22.8 %copy-start.6 = (s32[64]{0:T(128)S(1)}, s32[64]{0:T(128)}, u32[]{:S(2)}) copy-start(s32[64]{0:T(128)} %eq.51) | copy-start | bytes 772
  268.0 1.3 collective-permute-start.2
  270.6 3.6 %collective-permute-start.3 = (f32[1]{0:T(128)}, f32[1]{0:T(128)}, u32[]{:S(2)}, u32[]{:S(2)}) collective-permute-start(f32[1]{0:T(128)} %add.79), channel_id=1, source_target_pairs={{0,2},{2,0},{1,3},{3,1},{4,6},{6,4},{5,7},{7,5},{8,10},{10,8},{9,1... | collective-permute-start | bytes 20 | tf_op jit(solution)/shard_map/ppermute | solution.py:24
